TPU v7x, 32 devices: a whole 2x2x4 slice. The times are simulated.
32 devices in a mesh: dom: 2 (over y), wide: 16 (over z, x, core).
Axes of the slice: x: 2, y: 2, z: 4, core: 2. Of those that a mesh axis runs over, the one named last changes fastest.
Arguments:
- embeddings: bfloat16 [16384, 768], P(('dom', 'wide')), parts along dimension 0, may hold values from -6 to 6
- cluster_id: int32 [16384, 1], P(('dom', 'wide')), parts along dimension 0, may hold values from 0 to 7; in each aligned block of 512 rows (0 to 511, 512 to 1023, ...) at most 160 rows name the same one
Outputs:
- max_similarity: float32 [16384], P(('dom', 'wide')), parts along dimension 0
There are 2 independent parts, one for each index of `dom`. A program takes and returns all parts, laid end to end along the dimension named above; each array names one. Nothing has to cross between parts.
Inputs may be any that keep to these rules, and one draw needn't show every extreme that they name: `cluster_id`: among the 512 rows of one device (aligned blocks of 512 rows), no cluster appears more than 160 times; every cluster has some row.
All inputs are finite; a program needn't handle non-finite values.
Results may differ from a plain program's by a relative error of at most 0.0014.
Values may be sent and summed in bfloat16 or wider, within the bound.
A program may use at most 64 MiB of HBM per device.

v0:
```python
import math
import jax
import jax.numpy as jnp
from jax import lax
from jax.sharding import PartitionSpec as P


def swapped(value, axis, bit):
    mask = 2**bit
    pairs = [(source, source ^ mask) for source in range(lax.axis_size(axis))]
    return lax.ppermute(value, axis, pairs)


def normalize(embedded):
    values = embedded.astype(jnp.float32)
    inverse = lax.rsqrt(jnp.mean(values * values, axis=1, keepdims=True) + 1e-06)
    return (values * inverse * (1.0 / math.sqrt(values.shape[1]))).astype(jnp.bfloat16)


def pair_scores(queries, key_rows):
    return jnp.einsum("qd,kd->qk", queries, key_rows, preferred_element_type=jnp.float32)


def masked_max(scores, allowed):
    return jnp.max(jnp.where(allowed, scores, -1.0), axis=1)


def per_device(embeddings, cluster_id):
    axis_size = lax.axis_size("wide")
    rows_dev = embeddings.shape[0]
    feature_dim = embeddings.shape[1]
    clusters = axis_size // 2
    capacity = (5 * rows_dev + 2 * axis_size - 1) // (2 * axis_size)
    buffer_rows = axis_size * capacity
    unit_rows = normalize(embeddings)
    labels = cluster_id[:, 0]
    my_index = lax.axis_index("wide")
    my_flip = my_index % 2
    position = lax.iota(jnp.int32, rows_dev)
    same_cluster = labels[:, None] == labels[None, :]
    earlier = position[None, :] < position[:, None]
    local_rank = jnp.sum((same_cluster & earlier).astype(jnp.int32), axis=1)
    target = 2 * labels + (local_rank + my_flip) % 2
    slot_index = target * capacity + local_rank // 2
    outgoing = jnp.zeros((buffer_rows, feature_dim), jnp.bfloat16).at[slot_index].set(unit_rows)
    cluster_count = jnp.sum(
        (labels[:, None] == lax.iota(jnp.int32, clusters)[None, :]).astype(jnp.int32), axis=0
    )
    parity = lax.iota(jnp.int32, axis_size) % 2
    send_count = (jnp.repeat(cluster_count, 2) + 1 - (parity + my_flip) % 2) // 2
    outgoing_blocks = outgoing.reshape(axis_size, capacity, feature_dim)
    count_blocks = send_count.reshape(axis_size, 1)
    received, counts = (
        lax.all_to_all(outgoing_blocks, "wide", split_axis=0, concat_axis=0, tiled=True),
        lax.all_to_all(count_blocks, "wide", split_axis=0, concat_axis=0, tiled=True),
    )
    own_rows = received.reshape(buffer_rows, feature_dim)
    partner, partner_counts = swapped((own_rows, counts), "wide", 0)
    side_bit = my_index % 2
    slot_pos = lax.iota(jnp.int32, capacity)
    sources = lax.iota(jnp.int32, axis_size)
    base_key = (sources[:, None] * (2 * capacity) + 2 * slot_pos[None, :]).reshape(-1)
    source_parity = jnp.repeat(sources % 2, capacity)
    own_key = base_key + (side_bit + source_parity) % 2
    partner_key = base_key + (1 - side_bit + source_parity) % 2
    own_live = (slot_pos[None, :] < counts).reshape(-1)
    partner_live = (slot_pos[None, :] < partner_counts).reshape(-1)
    blocks = 8
    query_rows = own_rows.reshape(blocks, -1, feature_dim)
    query_key = own_key.reshape(blocks, -1)

    def self_max(pieces):
        queries, keys_here = pieces
        return masked_max(
            pair_scores(queries, own_rows),
            own_live[None, :] & (own_key[None, :] < keys_here[:, None]),
        )

    self_best = lax.map(self_max, (query_rows, query_key)).reshape(-1)
    first = side_bit == 0
    left_rows = jnp.where(first, own_rows, partner)
    left_key = jnp.where(first, own_key, partner_key)
    left_live = jnp.where(first, own_live, partner_live)
    right_rows = jnp.where(first, partner, own_rows)
    right_key = jnp.where(first, partner_key, own_key)
    right_live = jnp.where(first, partner_live, own_live)
    half_rows = buffer_rows // 2
    start = side_bit * half_rows
    lower_rows = lax.dynamic_slice_in_dim(left_rows, start, half_rows, 0).reshape(
        blocks // 2, -1, feature_dim
    )
    lower_key = lax.dynamic_slice_in_dim(left_key, start, half_rows, 0).reshape(blocks // 2, -1)
    lower_live = lax.dynamic_slice_in_dim(left_live, start, half_rows, 0).reshape(blocks // 2, -1)

    def cross_max(pieces):
        queries, keys_here, live_here = pieces
        scores = pair_scores(queries, right_rows)
        row_best = masked_max(
            scores, right_live[None, :] & (right_key[None, :] < keys_here[:, None])
        )
        column_mask = live_here[:, None] & (keys_here[:, None] < right_key[None, :])
        column_best = jnp.max(jnp.where(column_mask, scores, -1.0), axis=0)
        return (row_best, column_best)

    row_best, column_best = lax.map(cross_max, (lower_rows, lower_key, lower_live))
    row_best = row_best.reshape(-1)
    column_best = jnp.max(column_best, axis=0)
    placed = lax.dynamic_update_slice_in_dim(
        jnp.full((buffer_rows,), -1.0, jnp.float32), row_best, start, 0
    )
    kept = jnp.where(first, placed, column_best)
    handed = jnp.where(first, column_best, placed)
    returned = swapped(handed, "wide", 0)
    best_all = jnp.maximum(self_best, jnp.maximum(kept, returned))
    back = lax.all_to_all(
        best_all.reshape(axis_size, capacity), "wide", split_axis=0, concat_axis=0, tiled=True
    )
    return back.reshape(-1)[slot_index]


def solution(mesh):
    placed = (P(("dom", "wide"), None), P(("dom", "wide"), None))
    return jax.shard_map(
        per_device, mesh=mesh, in_specs=placed, out_specs=P(("dom", "wide")), check_vma=False
    )
```

profile of v0, /device:TPU:0, one launch (start us, length us, event | category | flops | bytes accessed | tf_op | source)
XLA Modules:
  0.0 119.5 jit_solution(761466265437939160)
XLA Ops:
  0.0 1.0 convert_reduce_fusion
  1.0 1.4 %fusion.24 = f32[512]{0:T(512)S(1)} fusion(bf16[512,768]{1,0:T(8,128)(2,1)} %param.6), kind=kLoop, calls=%fused_computation.45 | loop fusion | flops 1179136 | bytes 788480 | tf_op jit(solution)/shard_map/reduce_sum | solution.py:16
  2.4 0.7 compare_select_fusion
  3.1 4.7 %scatter_custom_fusion = bf16[1280,768]{1,0:T(8,128)(2,1)} fusion(s32[512]{0:T(512)S(1)} %bitcast.57, bf16[]{:T(256)} %constant.137.clone.1, bf16[512,768]{1,0:T(8,128)(2,1)} %param.6, f32[]{:T(128)} %constant.146.clone.1, f32[512]{0:T(512)S(1)} %add_rsqrt_fusion), kind=kCustom, calls=%fused_computation.52 | custom fusion | flops 1572864 | bytes 2754566 | tf_op jit(solution)/shard_map/scatter | solution.py:45
  7.8 7.5 %all-to-all-start.1 = ((bf16[16,80,768]{2,1,0:T(8,128)(2,1)}), bf16[16,80,768]{2,1,0:T(8,128)(2,1)S(1)}, u32[]{:S(2)}, u32[]{:S(2)}) async-start(bf16[16,80,768]{2,1,0:T(8,128)(2,1)} %bitcast.46), calls=%async_computation.1 | async-start | bytes 3932160 | tf_op jit(solution)/shard_map/all_to_all | solution.py:54
  15.6 0.1 add.278
  15.7 0.1 convert_reduce_fusion.1
  15.9 0.1 add.240
  16.0 0.7 copy.5
  16.7 37.4 %all-to-all-done.1 = bf16[16,80,768]{2,1,0:T(8,128)(2,1)S(1)} async-done(((bf16[16,80,768]{2,1,0:T(8,128)(2,1)}), bf16[16,80,768]{2,1,0:T(8,128)(2,1)S(1)}, u32[]{:S(2)}, u32[]{:S(2)}) %all-to-all-start.1) | async-done | bytes 1966112 | tf_op jit(solution)/shard_map/all_to_all | solution.py:54
  54.0 10.7 %all-to-all-start = ((s32[16,1,1]{2,1,0:T(1,128)}), s32[16,1,1]{2,1,0:T(1,128)S(1)}, u32[]{:S(2)}, u32[]{:S(2)}) async-start(s32[16,1,1]{2,1,0:T(1,128)} %copy.5), calls=%async_computation | async-start | bytes 16384 | tf_op jit(solution)/shard_map/all_to_all | solution.py:55
  64.7 0.4 collective-permute-start.1
  65.4 0.1 add.265
  65.5 0.1 add.259
  65.6 0.1 add.257
  65.8 0.1 fusion.39
  65.9 5.3 %all-to-all-done = s32[16,1,1]{2,1,0:T(1,128)S(1)} async-done(((s32[16,1,1]{2,1,0:T(1,128)}), s32[16,1,1]{2,1,0:T(1,128)S(1)}, u32[]{:S(2)}, u32[]{:S(2)}) %all-to-all-start) | async-done | bytes 96 | tf_op jit(solution)/shard_map/all_to_all | solution.py:55
  71.2 0.4 reduce.1
  71.6 0.1 reshape.309
  71.7 1.1 collective-permute-done
  72.8 0.1 select_n.191
  72.9 0.1 dynamic_slice.31
  73.0 0.1 reshape.311
  73.1 3.0 %broadcast_select_fusion = bf16[1280,768]{1,0:T(8,128)(2,1)} fusion(bf16[1280,768]{1,0:T(8,128)(2,1)} %collective-permute-done.1, pred[]{:T(512)} %eq.50, bf16[16,80,768]{2,1,0:T(8,128)(2,1)S(1)} %all-to-all-done.1), kind=kLoop, calls=%fused_computation.44 | loop fusion | flops 983040 | bytes 5898241 | tf_op jit(solution)/shard_map/jit(_where)/select_n | solution.py:84
  76.1 1.4 %dynamic-slice_select_fusion = bf16[640,768]{1,0:T(8,128)(2,1)S(1)} fusion(bf16[1280,768]{1,0:T(8,128)(2,1)} %collective-permute-done.1, s32[]{:T(128)S(6)} %select_n.186, bf16[1280,768]{1,0:T(8,128)(2,1)S(1)} %bitcast.41, pred[]{:T(512)} %eq.50), kind=kLoop, calls=%fused_computation.51 | loop fusion | flops 491520 | bytes 2949125 | tf_op jit(solution)/shard_map/jit(_where)/select_n | solution.py:81
  77.6 13.4 %while.26 = (s32[]{:T(128)}, f32[4,160]{1,0:T(4,128)S(1)}, f32[4,1280]{1,0:T(4,128)S(1)}, s32[4,160]{1,0:T(4,128)S(1)}, bf16[4,160,768]{2,1,0:T(8,128)(2,1)S(1)}...) while((s32[]{:T(128)}, f32[4,160]{1,0:T(4,128)S(1)}, ...), condition=%wide.region_10.11_spmd.clone.clone, body=%wide.region_7.10_spmd.clone.clone.sunk | while | flops 316246880 | bytes 2323947 | solution.py:105
  77.7 0.1 add.781
  78.2 0.1 select_n.336
  78.3 2.5 %select_reduce_fusion.3 = (f32[1280]{0:T(1024)S(1)}, f32[160]{0:T(256)S(1)}) fusion(s32[1280]{0:T(1024)S(1)} %fusion.69, s32[160]{0:T(256)S(1)} %bitcast.54, pred[160]{0:T(512)(128)(4,1)S(1)} %dynamic-slice_reduce_fusion.2, pred[1280]{0:T(1024)(128)(4,1)S(1)} %select_n.336, bf16[1280,768]{1,0:T(8,128)(2,1)} %get-tuple-element.460, ...), kind=kOutput, calls=%fused_computation.19.clone.1 | convolution fusion | flops 316209760 | bytes 2229380 | tf_op jit(solution)/shard_map/while/body/eval_jaxpr/qd,kd->qk/dot_general | solution.py:21
  80.8 0.1 dynamic_update_slice.26
  81.5 0.1 select_n.336
  81.6 2.5 %select_reduce_fusion.3 = (f32[1280]{0:T(1024)S(1)}, f32[160]{0:T(256)S(1)}) fusion(s32[1280]{0:T(1024)S(1)} %fusion.69, s32[160]{0:T(256)S(1)} %bitcast.54, pred[160]{0:T(512)(128)(4,1)S(1)} %dynamic-slice_reduce_fusion.2, pred[1280]{0:T(1024)(128)(4,1)S(1)} %select_n.336, bf16[1280,768]{1,0:T(8,128)(2,1)} %get-tuple-element.460, ...), kind=kOutput, calls=%fused_computation.19.clone.1 | convolution fusion | flops 316209760 | bytes 2229380 | tf_op jit(solution)/shard_map/while/body/eval_jaxpr/qd,kd->qk/dot_general | solution.py:21
  84.1 0.1 dynamic_update_slice.26
  84.9 0.1 select_n.336
  85.0 2.5 %select_reduce_fusion.3 = (f32[1280]{0:T(1024)S(1)}, f32[160]{0:T(256)S(1)}) fusion(s32[1280]{0:T(1024)S(1)} %fusion.69, s32[160]{0:T(256)S(1)} %bitcast.54, pred[160]{0:T(512)(128)(4,1)S(1)} %dynamic-slice_reduce_fusion.2, pred[1280]{0:T(1024)(128)(4,1)S(1)} %select_n.336, bf16[1280,768]{1,0:T(8,128)(2,1)} %get-tuple-element.460, ...), kind=kOutput, calls=%fused_computation.19.clone.1 | convolution fusion | flops 316209760 | bytes 2229380 | tf_op jit(solution)/shard_map/while/body/eval_jaxpr/qd,kd->qk/dot_general | solution.py:21
  87.5 0.1 dynamic_update_slice.26
  88.2 0.1 select_n.336
  88.3 2.5 %select_reduce_fusion.3 = (f32[1280]{0:T(1024)S(1)}, f32[160]{0:T(256)S(1)}) fusion(s32[1280]{0:T(1024)S(1)} %fusion.69, s32[160]{0:T(256)S(1)} %bitcast.54, pred[160]{0:T(512)(128)(4,1)S(1)} %dynamic-slice_reduce_fusion.2, pred[1280]{0:T(1024)(128)(4,1)S(1)} %select_n.336, bf16[1280,768]{1,0:T(8,128)(2,1)} %get-tuple-element.460, ...), kind=kOutput, calls=%fused_computation.19.clone.1 | convolution fusion | flops 316209760 | bytes 2229380 | tf_op jit(solution)/shard_map/while/body/eval_jaxpr/qd,kd->qk/dot_general | solution.py:21
  90.8 0.1 dynamic_update_slice.26
  91.0 0.1 reshape.312
  91.1 0.3 dynamic_update_slice.15
  91.4 11.8 %while.25 = (s32[]{:T(128)}, f32[8,160]{1,0:T(8,128)S(1)}, s32[8,160]{1,0:T(8,128)S(1)}, bf16[8,160,768]{2,1,0:T(8,128)(2,1)S(1)}, bf16[1280,768]{1,0:T(8,128)(2...) while((s32[]{:T(128)}, f32[8,160]{1,0:T(8,128)S(1)}, ...), condition=%wide.region_6.7_spmd.clone, body=%wide.region_4.6_spmd.clone.sunk | while | flops 315409760 | bytes 2276857 | solution.py:79
  91.8 0.1 and.250
  91.9 0.9 fusion.67
  93.3 0.1 and.250
  93.4 0.9 fusion.67
  94.8 0.1 and.250
  94.9 0.9 fusion.67
  96.3 0.1 and.250
  96.4 0.9 fusion.67
  97.8 0.1 and.250
  97.9 0.9 fusion.67
  99.2 0.1 and.250
  99.3 0.9 fusion.67
  100.7 0.1 and.250
  100.8 0.9 fusion.67
  102.2 0.1 and.250
  102.3 0.9 fusion.67
  103.4 0.7 all_to_all.18
  104.1 3.5 %all-to-all-start.2 = ((f32[16,1,80]{2,1,0:T(1,128)}), f32[16,1,80]{2,1,0:T(1,128)S(1)}, u32[]{:S(2)}, u32[]{:S(2)}) async-start(f32[16,1,80]{2,1,0:T(1,128)} %all_to_all.18), calls=%async_computation.2 | async-start | bytes 16384 | tf_op jit(solution)/shard_map/all_to_all | solution.py:115
  107.6 6.4 %all-to-all-done.2 = f32[16,1,80]{2,1,0:T(1,128)S(1)} async-done(((f32[16,1,80]{2,1,0:T(1,128)}), f32[16,1,80]{2,1,0:T(1,128)S(1)}, u32[]{:S(2)}, u32[]{:S(2)}) %all-to-all-start.2) | async-done | bytes 5152 | tf_op jit(solution)/shard_map/all_to_all | solution.py:115
  114.0 0.5 broadcast.407
  114.5 0.7 reduce.7
  115.2 4.3 %gather_fusion = f32[512]{0:T(512)} fusion(f32[1280]{0:T(1024)S(1)} %reshape.313, s32[1024]{0:T(1024)S(1)} %pad_clamp_fusion), kind=kCustom, calls=%fused_computation | custom fusion | bytes 6144 | tf_op jit(solution)/shard_map/gather | solution.py:118
  (150 shorter events, 7.0 us)
Async XLA Ops:
  7.8 7.9 %copy-start = (s32[512,1]{0,1:T(1,128)S(1)}, s32[512,1]{0,1:T(1,128)}, u32[]{:S(2)}) copy-start(s32[512,1]{0,1:T(1,128)} %param.7) | copy-start | bytes 6148
  7.8 46.2 %all-to-all-start.1 = ((bf16[16,80,768]{2,1,0:T(8,128)(2,1)}), bf16[16,80,768]{2,1,0:T(8,128)(2,1)S(1)}, u32[]{:S(2)}, u32[]{:S(2)}) async-start(bf16[16,80,768]{2,1,0:T(8,128)(2,1)} %bitcast.46), calls=%async_computation.1 | async-start | bytes 3932160 | tf_op jit(solution)/shard_map/all_to_all | solution.py:54
  54.0 17.1 %all-to-all-start = ((s32[16,1,1]{2,1,0:T(1,128)}), s32[16,1,1]{2,1,0:T(1,128)S(1)}, u32[]{:S(2)}, u32[]{:S(2)}) async-start(s32[16,1,1]{2,1,0:T(1,128)} %copy.5), calls=%async_computation | async-start | bytes 16384 | tf_op jit(solution)/shard_map/all_to_all | solution.py:55
  64.7 8.4 %collective-permute-start.1 = (bf16[1280,768]{1,0:T(8,128)(2,1)S(1)}, bf16[1280,768]{1,0:T(8,128)(2,1)}, u32[]{:S(2)}, u32[]{:S(2)}) collective-permute-start(bf16[1280,768]{1,0:T(8,128)(2,1)S(1)} %bitcast.40), channel_id=1, source_target_pairs={{0,1},{1,0},{2,3},{3,2},{4,5},{5,4},{6,7},{7,6},{8,9},{9,8},{10,11... | collective-permute-start | bytes 5898248 | tf_op jit(solution)/shard_map/ppermute | solution.py:11
  71.5 1.2 %collective-permute-start = (s32[16,1]{0,1:T(1,128)S(1)}, s32[16,1]{0,1:T(1,128)S(1)}, u32[]{:S(2)}, u32[]{:S(2)}) collective-permute-start(s32[16,1]{0,1:T(1,128)S(1)} %bitcast.48), channel_id=1, source_target_pairs={{0,1},{1,0},{2,3},{3,2},{4,5},{5,4},{6,7},{7,6},{8,9},{9,8},{10,11... | collective-permute-start | bytes 200 | tf_op jit(solution)/shard_map/ppermute | solution.py:11
  91.3 12.0 %collective-permute-start.2 = (f32[1280]{0:T(1024)S(1)}, f32[1280]{0:T(1024)S(1)}, u32[]{:S(2)}, u32[]{:S(2)}) collective-permute-start(f32[1280]{0:T(1024)S(1)} %broadcast_select_fusion.1), channel_id=1, source_target_pairs={{0,1},{1,0},{2,3},{3,2},{4,5},{5,4},{6,7},{7,6},{8,9},{9,8},{10,11... | collective-permute-start | bytes 15368 | tf_op jit(solution)/shard_map/ppermute | solution.py:11
  104.1 9.9 %all-to-all-start.2 = ((f32[16,1,80]{2,1,0:T(1,128)}), f32[16,1,80]{2,1,0:T(1,128)S(1)}, u32[]{:S(2)}, u32[]{:S(2)}) async-start(f32[16,1,80]{2,1,0:T(1,128)} %all_to_all.18), calls=%async_computation.2 | async-start | bytes 16384 | tf_op jit(solution)/shard_map/all_to_all | solution.py:115
where the time goes:
time: 120 us; the launch traced here: 119 us
  waiting for transfers between devices  50.1 us (42%)
  starting transfers between devices  22.2 us (18%)
  matrix products  17.4 us (14%)
  other arithmetic  15.8 us (13%)
  local copies, waits for them, and re-layouts  13.3 us (11%)
    all_to_all x1, waiting for transfers between devices, per_device(): lax.all_to_all(outgoing_blocks, 'wide', split_axis=0, concat_axis=0, tile...  37.4 us
    dot_general x12, matrix products, pair_scores(): jnp.einsum('qd,kd->qk', queries, key_rows, preferred_element_type=jnp.flo...  17.4 us
    all_to_all x1, starting transfers between devices, per_device(): lax.all_to_all(count_blocks, 'wide', split_axis=0, concat_axis=0, tiled=T...  10.7 us
    all_to_all x1, starting transfers between devices, per_device(): lax.all_to_all(outgoing_blocks, 'wide', split_axis=0, concat_axis=0, tile...  7.52 us
    all_to_all x1, waiting for transfers between devices, per_device(): lax.all_to_all(best_all.reshape(axis_size, capacity), 'wide', split_axis=...  6.38 us
    all_to_all x1, waiting for transfers between devices, per_device(): lax.all_to_all(count_blocks, 'wide', split_axis=0, concat_axis=0, tiled=T...  5.28 us
    scatter x1, other arithmetic, per_device(): jnp.zeros((buffer_rows, feature_dim), jnp.bfloat16).at[slot_index]  4.71 us
    gather x1, local copies, waits for them, and re-layouts, per_device(): return back.reshape(-1)[slot_index]  4.27 us
  transfers between devices with their start and end apart: 6, of which 4 were waited for; matrix products, arithmetic and copies ran while one was open for 12% of the time, Pallas kernels for 0%

commit v1 on v0

--- a/solution.py
+++ b/solution.py
@@ -3,6 +3,18 @@
 import jax.numpy as jnp
 from jax import lax
 from jax.sharding import PartitionSpec as P
+
+
+def in_blocks(x, dim, size):
+    dims = x.shape
+    tiles = x.reshape(*dims[:dim], size, dims[dim] // size, *dims[dim + 1 :])
+    return jnp.moveaxis(tiles, dim, 0)
+
+
+def laid_out(blocks, dim):
+    blocks = jnp.moveaxis(blocks, 0, dim)
+    shape = blocks.shape
+    return blocks.reshape(*shape[:dim], shape[dim] * shape[dim + 1], *shape[dim + 2 :])
 
 
 def swapped(value, axis, bit):
@@ -112,9 +124,15 @@
     handed = jnp.where(first, column_best, placed)
     returned = swapped(handed, "wide", 0)
     best_all = jnp.maximum(self_best, jnp.maximum(kept, returned))
-    back = lax.all_to_all(
-        best_all.reshape(axis_size, capacity), "wide", split_axis=0, concat_axis=0, tiled=True
-    )
+    shard = best_all.reshape(axis_size, capacity)
+    count, mine = (lax.axis_size("wide"), lax.axis_index("wide"))
+    parts = in_blocks(shard, 0, count)
+    outs = [parts[mine]]
+    for turn in range(1, count):
+        sent = parts[mine ^ turn]
+        outs.append(lax.ppermute(sent, "wide", [(i, i ^ turn) for i in range(count)]))
+    parts = jnp.stack(outs)[mine ^ jnp.arange(count)]
+    back = laid_out(parts, 0)
     return back.reshape(-1)[slot_index]
 
 

time: 120 us -> 132 us (1.10)
  starting transfers between devices: 22.2 us -> 39.3 us
  waiting for transfers between devices: 50.1 us -> 45.9 us
    ppermute x0 -> x15, starting transfers between devices: none -> 20.5 us  [per_device(): lax.ppermute(sent, 'wide', [(i, i ^ turn) for i in range(count)])]
    all_to_all x1 -> x0, waiting for transfers between devices: 6.38 us -> none  [per_device(): lax.all_to_all(best_all.reshape(axis_size, capacity), 'wide', split_axis=...]
    all_to_all x1 -> x0, starting transfers between devices: 3.49 us -> none  [per_device(): lax.all_to_all(best_all.reshape(axis_size, capacity), 'wide', split_axis=...]
    ppermute x0 -> x15, waiting for transfers between devices: none -> 2.26 us  [per_device(): lax.ppermute(sent, 'wide', [(i, i ^ turn) for i in range(count)])]
  transfers between devices with their start and end apart: 6 -> 20, of which waited for: 4 -> 5; matrix products, arithmetic and copies ran while one was open for 12% -> 11% of each run, Pallas kernels for 0% -> 0%
where the time goes in v1:
time: 132 us; the launch traced here: 131 us
  waiting for transfers between devices  45.9 us (35%)
  starting transfers between devices  39.3 us (30%)
  matrix products  17.4 us (13%)
  other arithmetic  15.1 us (11%)
  local copies, waits for them, and re-layouts  12.8 us (10%)
    all_to_all x1, waiting for transfers between devices, per_device(): lax.all_to_all(outgoing_blocks, 'wide', split_axis=0, concat_axis=0, tile...  37.4 us
    ppermute x15, starting transfers between devices, per_device(): lax.ppermute(sent, 'wide', [(i, i ^ turn) for i in range(count)])  20.5 us
    dot_general x12, matrix products, pair_scores(): jnp.einsum('qd,kd->qk', queries, key_rows, preferred_element_type=jnp.flo...  17.4 us
    all_to_all x1, starting transfers between devices, per_device(): lax.all_to_all(count_blocks, 'wide', split_axis=0, concat_axis=0, tiled=T...  10.7 us
    all_to_all x1, starting transfers between devices, per_device(): lax.all_to_all(outgoing_blocks, 'wide', split_axis=0, concat_axis=0, tile...  7.52 us
    all_to_all x1, waiting for transfers between devices, per_device(): lax.all_to_all(count_blocks, 'wide', split_axis=0, concat_axis=0, tiled=T...  5.01 us
    scatter x1, other arithmetic, per_device(): jnp.zeros((buffer_rows, feature_dim), jnp.bfloat16).at[slot_index]  4.71 us
    gather x1, local copies, waits for them, and re-layouts, per_device(): return back.reshape(-1)[slot_index]  4.27 us
  transfers between devices with their start and end apart: 20, of which 5 were waited for; matrix products, arithmetic and copies ran while one was open for 11% of the time, Pallas kernels for 0%

profile of v1, /device:TPU:0, one launch (start us, length us, event | category | flops | bytes accessed | tf_op | source)
XLA Modules:
  0.0 131.3 jit_solution(1628581214497553064)
XLA Ops:
  0.0 1.0 convert_reduce_fusion
  1.0 1.4 %fusion.24 = f32[512]{0:T(512)S(1)} fusion(bf16[512,768]{1,0:T(8,128)(2,1)} %param.6), kind=kLoop, calls=%fused_computation.46 | loop fusion | flops 1179136 | bytes 788480 | tf_op jit(solution)/shard_map/reduce_sum | solution.py:28
  2.4 0.7 compare_select_fusion
  3.1 4.7 %scatter_custom_fusion = bf16[1280,768]{1,0:T(8,128)(2,1)} fusion(s32[512]{0:T(512)S(1)} %bitcast.136, bf16[]{:T(256)} %constant.153.clone.1, bf16[512,768]{1,0:T(8,128)(2,1)} %param.6, f32[]{:T(128)} %constant.162.clone.1, f32[512]{0:T(512)S(1)} %add_rsqrt_fusion), kind=kCustom, calls=%fused_computation.53 | custom fusion | flops 1572864 | bytes 2754566 | tf_op jit(solution)/shard_map/scatter | solution.py:57
  7.8 7.5 %all-to-all-start.1 = ((bf16[16,80,768]{2,1,0:T(8,128)(2,1)}), bf16[16,80,768]{2,1,0:T(8,128)(2,1)S(1)}, u32[]{:S(2)}, u32[]{:S(2)}) async-start(bf16[16,80,768]{2,1,0:T(8,128)(2,1)} %bitcast.124), calls=%async_computation.1 | async-start | bytes 3932160 | tf_op jit(solution)/shard_map/all_to_all | solution.py:66
  15.6 0.1 convert_reduce_fusion.1
  15.9 0.7 copy.65
  16.6 37.4 %all-to-all-done.1 = bf16[16,80,768]{2,1,0:T(8,128)(2,1)S(1)} async-done(((bf16[16,80,768]{2,1,0:T(8,128)(2,1)}), bf16[16,80,768]{2,1,0:T(8,128)(2,1)S(1)}, u32[]{:S(2)}, u32[]{:S(2)}) %all-to-all-start.1) | async-done | bytes 1966112 | tf_op jit(solution)/shard_map/all_to_all | solution.py:66
  54.0 10.7 %all-to-all-start = ((s32[16,1,1]{2,1,0:T(1,128)}), s32[16,1,1]{2,1,0:T(1,128)S(1)}, u32[]{:S(2)}, u32[]{:S(2)}) async-start(s32[16,1,1]{2,1,0:T(1,128)} %copy.65), calls=%async_computation | async-start | bytes 16384 | tf_op jit(solution)/shard_map/all_to_all | solution.py:67
  64.7 0.4 collective-permute-start.1
  66.1 5.0 %all-to-all-done = s32[16,1,1]{2,1,0:T(1,128)S(1)} async-done(((s32[16,1,1]{2,1,0:T(1,128)}), s32[16,1,1]{2,1,0:T(1,128)S(1)}, u32[]{:S(2)}, u32[]{:S(2)}) %all-to-all-start) | async-done | bytes 96 | tf_op jit(solution)/shard_map/all_to_all | solution.py:67
  71.2 0.4 reduce.1
  71.6 1.1 collective-permute-done
  72.8 0.1 select_n.249
  73.0 0.1 reshape.319
  73.1 3.0 %broadcast_select_fusion = bf16[1280,768]{1,0:T(8,128)(2,1)} fusion(bf16[1280,768]{1,0:T(8,128)(2,1)} %collective-permute-done.1, pred[]{:T(512)} %eq.50, bf16[16,80,768]{2,1,0:T(8,128)(2,1)S(1)} %all-to-all-done.1), kind=kLoop, calls=%fused_computation.45 | loop fusion | flops 983040 | bytes 5898241 | tf_op jit(solution)/shard_map/jit(_where)/select_n | solution.py:96
  76.1 1.4 %dynamic-slice_select_fusion = bf16[640,768]{1,0:T(8,128)(2,1)S(1)} fusion(bf16[1280,768]{1,0:T(8,128)(2,1)} %collective-permute-done.1, s32[]{:T(128)S(6)} %select_n.244, bf16[1280,768]{1,0:T(8,128)(2,1)S(1)} %bitcast.119, pred[]{:T(512)} %eq.50), kind=kLoop, calls=%fused_computation.52 | loop fusion | flops 491520 | bytes 2949125 | tf_op jit(solution)/shard_map/jit(_where)/select_n | solution.py:93
  77.6 13.4 %while.26 = (s32[]{:T(128)}, f32[4,160]{1,0:T(4,128)S(1)}, f32[4,1280]{1,0:T(4,128)S(1)}, s32[4,160]{1,0:T(4,128)S(1)}, bf16[4,160,768]{2,1,0:T(8,128)(2,1)S(1)}...) while((s32[]{:T(128)}, f32[4,160]{1,0:T(4,128)S(1)}, ...), condition=%wide.region_10.11_spmd.clone.clone, body=%wide.region_7.10_spmd.clone.clone.sunk | while | flops 316246880 | bytes 2323947 | solution.py:117
  78.2 0.1 select_n.414
  78.3 2.5 %select_reduce_fusion.3 = (f32[1280]{0:T(1024)S(1)}, f32[160]{0:T(256)S(1)}) fusion(s32[1280]{0:T(1024)S(1)} %fusion.85, s32[160]{0:T(256)S(1)} %bitcast.133, pred[160]{0:T(512)(128)(4,1)S(1)} %dynamic-slice_reduce_fusion.2, pred[1280]{0:T(1024)(128)(4,1)S(1)} %select_n.414, bf16[1280,768]{1,0:T(8,128)(2,1)} %get-tuple-element.478, ...), kind=kOutput, calls=%fused_computation.20.clone.1 | convolution fusion | flops 316209760 | bytes 2229380 | tf_op jit(solution)/shard_map/while/body/eval_jaxpr/qd,kd->qk/dot_general | solution.py:33
  81.5 0.1 select_n.414
  81.6 2.5 %select_reduce_fusion.3 = (f32[1280]{0:T(1024)S(1)}, f32[160]{0:T(256)S(1)}) fusion(s32[1280]{0:T(1024)S(1)} %fusion.85, s32[160]{0:T(256)S(1)} %bitcast.133, pred[160]{0:T(512)(128)(4,1)S(1)} %dynamic-slice_reduce_fusion.2, pred[1280]{0:T(1024)(128)(4,1)S(1)} %select_n.414, bf16[1280,768]{1,0:T(8,128)(2,1)} %get-tuple-element.478, ...), kind=kOutput, calls=%fused_computation.20.clone.1 | convolution fusion | flops 316209760 | bytes 2229380 | tf_op jit(solution)/shard_map/while/body/eval_jaxpr/qd,kd->qk/dot_general | solution.py:33
  84.1 0.1 dynamic_update_slice.26
  84.9 0.1 select_n.414
  85.0 2.5 %select_reduce_fusion.3 = (f32[1280]{0:T(1024)S(1)}, f32[160]{0:T(256)S(1)}) fusion(s32[1280]{0:T(1024)S(1)} %fusion.85, s32[160]{0:T(256)S(1)} %bitcast.133, pred[160]{0:T(512)(128)(4,1)S(1)} %dynamic-slice_reduce_fusion.2, pred[1280]{0:T(1024)(128)(4,1)S(1)} %select_n.414, bf16[1280,768]{1,0:T(8,128)(2,1)} %get-tuple-element.478, ...), kind=kOutput, calls=%fused_computation.20.clone.1 | convolution fusion | flops 316209760 | bytes 2229380 | tf_op jit(solution)/shard_map/while/body/eval_jaxpr/qd,kd->qk/dot_general | solution.py:33
  88.2 0.1 select_n.414
  88.3 2.5 %select_reduce_fusion.3 = (f32[1280]{0:T(1024)S(1)}, f32[160]{0:T(256)S(1)}) fusion(s32[1280]{0:T(1024)S(1)} %fusion.85, s32[160]{0:T(256)S(1)} %bitcast.133, pred[160]{0:T(512)(128)(4,1)S(1)} %dynamic-slice_reduce_fusion.2, pred[1280]{0:T(1024)(128)(4,1)S(1)} %select_n.414, bf16[1280,768]{1,0:T(8,128)(2,1)} %get-tuple-element.478, ...), kind=kOutput, calls=%fused_computation.20.clone.1 | convolution fusion | flops 316209760 | bytes 2229380 | tf_op jit(solution)/shard_map/while/body/eval_jaxpr/qd,kd->qk/dot_general | solution.py:33
  91.0 0.3 dynamic_update_slice.15
  91.4 11.8 %while.25 = (s32[]{:T(128)}, f32[8,160]{1,0:T(8,128)S(1)}, s32[8,160]{1,0:T(8,128)S(1)}, bf16[8,160,768]{2,1,0:T(8,128)(2,1)S(1)}, bf16[1280,768]{1,0:T(8,128)(2...) while((s32[]{:T(128)}, f32[8,160]{1,0:T(8,128)S(1)}, ...), condition=%wide.region_6.7_spmd.clone, body=%wide.region_4.6_spmd.clone.sunk | while | flops 315409760 | bytes 2276857 | solution.py:91
  91.8 0.1 and.250
  91.9 0.9 fusion.83
  93.3 0.1 and.250
  93.4 0.9 fusion.83
  94.8 0.1 and.250
  94.9 0.9 fusion.83
  96.3 0.1 and.250
  96.4 0.9 fusion.83
  97.8 0.1 and.250
  97.8 0.9 fusion.83
  99.2 0.1 and.250
  99.3 0.9 fusion.83
  100.7 0.1 and.250
  100.8 0.9 fusion.83
  102.2 0.1 and.250
  102.3 0.9 fusion.83
  103.5 0.5 collective-permute-start.3
  104.0 0.5 collective-permute-start.4
  104.5 0.9 collective-permute-start.5
  105.5 0.5 collective-permute-start.6
  106.0 1.5 %collective-permute-start.7 = (f32[1,80]{1,0:T(1,128)S(1)}, f32[1,80]{1,0:T(1,128)S(1)}, u32[]{:S(2)}, u32[]{:S(2)}) collective-permute-start(f32[1,80]{1,0:T(1,128)S(1)} %get-tuple-element.250), channel_id=1, source_target_pairs={{0,5},{1,4},{2,7},{3,6},{4,1},{5,0},{6,3},{7,2},{8,13},{9,12},{10,... | collective-permute-start | bytes 968 | tf_op jit(solution)/shard_map/ppermute | solution.py:133
  107.5 0.5 collective-permute-start.8
  108.1 1.8 %collective-permute-start.9 = (f32[1,80]{1,0:T(1,128)S(1)}, f32[1,80]{1,0:T(1,128)S(1)}, u32[]{:S(2)}, u32[]{:S(2)}) collective-permute-start(f32[1,80]{1,0:T(1,128)S(1)} %get-tuple-element.248), channel_id=1, source_target_pairs={{0,7},{1,6},{2,5},{3,4},{4,3},{5,2},{6,1},{7,0},{8,15},{9,14},{10,... | collective-permute-start | bytes 968 | tf_op jit(solution)/shard_map/ppermute | solution.py:133
  109.9 0.5 collective-permute-start.10
  110.4 2.4 %collective-permute-start.11 = (f32[1,80]{1,0:T(1,128)S(1)}, f32[1,80]{1,0:T(1,128)S(1)}, u32[]{:S(2)}, u32[]{:S(2)}) collective-permute-start(f32[1,80]{1,0:T(1,128)S(1)} %get-tuple-element.246), channel_id=1, source_target_pairs={{0,9},{1,8},{2,11},{3,10},{4,13},{5,12},{6,15},{7,14},{8,1},{9,0},... | collective-permute-start | bytes 968 | tf_op jit(solution)/shard_map/ppermute | solution.py:133
  112.8 0.5 collective-permute-start.12
  113.4 2.7 %collective-permute-start.13 = (f32[1,80]{1,0:T(1,128)S(1)}, f32[1,80]{1,0:T(1,128)S(1)}, u32[]{:S(2)}, u32[]{:S(2)}) collective-permute-start(f32[1,80]{1,0:T(1,128)S(1)} %get-tuple-element.244), channel_id=1, source_target_pairs={{0,11},{1,10},{2,9},{3,8},{4,15},{5,14},{6,13},{7,12},{8,3},{9,2},... | collective-permute-start | bytes 968 | tf_op jit(solution)/shard_map/ppermute | solution.py:133
  116.1 0.5 collective-permute-start.14
  116.6 3.3 %collective-permute-start.15 = (f32[1,80]{1,0:T(1,128)S(1)}, f32[1,80]{1,0:T(1,128)S(1)}, u32[]{:S(2)}, u32[]{:S(2)}) collective-permute-start(f32[1,80]{1,0:T(1,128)S(1)} %get-tuple-element.242), channel_id=1, source_target_pairs={{0,13},{1,12},{2,15},{3,14},{4,9},{5,8},{6,11},{7,10},{8,5},{9,4},... | collective-permute-start | bytes 968 | tf_op jit(solution)/shard_map/ppermute | solution.py:133
  119.9 0.7 collective-permute-start.16
  120.6 3.4 %collective-permute-start.17 = (f32[1,80]{1,0:T(1,128)S(1)}, f32[1,80]{1,0:T(1,128)S(1)}, u32[]{:S(2)}, u32[]{:S(2)}) collective-permute-start(f32[1,80]{1,0:T(1,128)S(1)} %get-tuple-element.240), channel_id=1, source_target_pairs={{0,15},{1,14},{2,13},{3,12},{4,11},{5,10},{6,9},{7,8},{8,7},{9,6},... | collective-permute-start | bytes 968 | tf_op jit(solution)/shard_map/ppermute | solution.py:133
  124.1 2.1 %collective-permute-done.16 = f32[1,80]{1,0:T(1,128)S(1)} collective-permute-done((f32[1,80]{1,0:T(1,128)S(1)}, f32[1,80]{1,0:T(1,128)S(1)}, u32[]{:S(2)}, u32[]{:S(2)}) %collective-permute-start.16) | collective-permute-done | bytes 352 | tf_op jit(solution)/shard_map/ppermute | solution.py:133
  126.2 0.1 collective-permute-done.17
  126.4 0.6 gather_fusion
  127.0 4.3 %gather_fusion.1 = f32[512]{0:T(512)} fusion(f32[1280]{0:T(1024)S(1)} %reshape_reshape.11, s32[1024]{0:T(1024)S(1)} %pad_clamp_fusion), kind=kCustom, calls=%fused_computation.1 | custom fusion | bytes 6144 | tf_op jit(solution)/shard_map/gather | solution.py:136
  (180 shorter events, 8.2 us)
Async XLA Ops:
  7.8 7.8 %copy-start = (s32[512,1]{0,1:T(1,128)S(1)}, s32[512,1]{0,1:T(1,128)}, u32[]{:S(2)}) copy-start(s32[512,1]{0,1:T(1,128)} %param.7) | copy-start | bytes 6148
  7.8 46.2 %all-to-all-start.1 = ((bf16[16,80,768]{2,1,0:T(8,128)(2,1)}), bf16[16,80,768]{2,1,0:T(8,128)(2,1)S(1)}, u32[]{:S(2)}, u32[]{:S(2)}) async-start(bf16[16,80,768]{2,1,0:T(8,128)(2,1)} %bitcast.124), calls=%async_computation.1 | async-start | bytes 3932160 | tf_op jit(solution)/shard_map/all_to_all | solution.py:66
  54.0 17.1 %all-to-all-start = ((s32[16,1,1]{2,1,0:T(1,128)}), s32[16,1,1]{2,1,0:T(1,128)S(1)}, u32[]{:S(2)}, u32[]{:S(2)}) async-start(s32[16,1,1]{2,1,0:T(1,128)} %copy.65), calls=%async_computation | async-start | bytes 16384 | tf_op jit(solution)/shard_map/all_to_all | solution.py:67
  64.7 8.4 %collective-permute-start.1 = (bf16[1280,768]{1,0:T(8,128)(2,1)S(1)}, bf16[1280,768]{1,0:T(8,128)(2,1)}, u32[]{:S(2)}, u32[]{:S(2)}) collective-permute-start(bf16[1280,768]{1,0:T(8,128)(2,1)S(1)} %bitcast.118), channel_id=1, source_target_pairs={{0,1},{1,0},{2,3},{3,2},{4,5},{5,4},{6,7},{7,6},{8,9},{9,8},{10,11... | collective-permute-start | bytes 5898248 | tf_op jit(solution)/shard_map/ppermute | solution.py:23
  71.5 1.2 collective-permute-start
  91.3 12.0 %collective-permute-start.2 = (f32[1280]{0:T(1024)S(1)}, f32[1280]{0:T(1024)S(1)}, u32[]{:S(2)}, u32[]{:S(2)}) collective-permute-start(f32[1280]{0:T(1024)S(1)} %broadcast_select_fusion.1), channel_id=1, source_target_pairs={{0,1},{1,0},{2,3},{3,2},{4,5},{5,4},{6,7},{7,6},{8,9},{9,8},{10,11... | collective-permute-start | bytes 15368 | tf_op jit(solution)/shard_map/ppermute | solution.py:23
  103.5 4.0 %collective-permute-start.3 = (f32[1,80]{1,0:T(1,128)S(1)}, f32[1,80]{1,0:T(1,128)S(1)}, u32[]{:S(2)}, u32[]{:S(2)}) collective-permute-start(f32[1,80]{1,0:T(1,128)S(1)} %get-tuple-element.254), channel_id=1, source_target_pairs={{0,1},{1,0},{2,3},{3,2},{4,5},{5,4},{6,7},{7,6},{8,9},{9,8},{10,11... | collective-permute-start | bytes 968 | tf_op jit(solution)/shard_map/ppermute | solution.py:133
  104.0 4.0 %collective-permute-start.4 = (f32[1,80]{1,0:T(1,128)S(1)}, f32[1,80]{1,0:T(1,128)S(1)}, u32[]{:S(2)}, u32[]{:S(2)}) collective-permute-start(f32[1,80]{1,0:T(1,128)S(1)} %get-tuple-element.253), channel_id=1, source_target_pairs={{0,2},{1,3},{2,0},{3,1},{4,6},{5,7},{6,4},{7,5},{8,10},{9,11},{10,... | collective-permute-start | bytes 968 | tf_op jit(solution)/shard_map/ppermute | solution.py:133
  104.5 5.3 %collective-permute-start.5 = (f32[1,80]{1,0:T(1,128)S(1)}, f32[1,80]{1,0:T(1,128)S(1)}, u32[]{:S(2)}, u32[]{:S(2)}) collective-permute-start(f32[1,80]{1,0:T(1,128)S(1)} %get-tuple-element.252), channel_id=1, source_target_pairs={{0,3},{1,2},{2,1},{3,0},{4,7},{5,6},{6,5},{7,4},{8,11},{9,10},{10,... | collective-permute-start | bytes 968 | tf_op jit(solution)/shard_map/ppermute | solution.py:133
  105.5 4.9 %collective-permute-start.6 = (f32[1,80]{1,0:T(1,128)S(1)}, f32[1,80]{1,0:T(1,128)S(1)}, u32[]{:S(2)}, u32[]{:S(2)}) collective-permute-start(f32[1,80]{1,0:T(1,128)S(1)} %get-tuple-element.251), channel_id=1, source_target_pairs={{0,4},{1,5},{2,6},{3,7},{4,0},{5,1},{6,2},{7,3},{8,12},{9,13},{10,... | collective-permute-start | bytes 968 | tf_op jit(solution)/shard_map/ppermute | solution.py:133
  106.0 6.9 %collective-permute-start.7 = (f32[1,80]{1,0:T(1,128)S(1)}, f32[1,80]{1,0:T(1,128)S(1)}, u32[]{:S(2)}, u32[]{:S(2)}) collective-permute-start(f32[1,80]{1,0:T(1,128)S(1)} %get-tuple-element.250), channel_id=1, source_target_pairs={{0,5},{1,4},{2,7},{3,6},{4,1},{5,0},{6,3},{7,2},{8,13},{9,12},{10,... | collective-permute-start | bytes 968 | tf_op jit(solution)/shard_map/ppermute | solution.py:133
  107.5 5.8 %collective-permute-start.8 = (f32[1,80]{1,0:T(1,128)S(1)}, f32[1,80]{1,0:T(1,128)S(1)}, u32[]{:S(2)}, u32[]{:S(2)}) collective-permute-start(f32[1,80]{1,0:T(1,128)S(1)} %get-tuple-element.249), channel_id=1, source_target_pairs={{0,6},{1,7},{2,4},{3,5},{4,2},{5,3},{6,0},{7,1},{8,14},{9,15},{10,... | collective-permute-start | bytes 968 | tf_op jit(solution)/shard_map/ppermute | solution.py:133
  108.1 8.0 %collective-permute-start.9 = (f32[1,80]{1,0:T(1,128)S(1)}, f32[1,80]{1,0:T(1,128)S(1)}, u32[]{:S(2)}, u32[]{:S(2)}) collective-permute-start(f32[1,80]{1,0:T(1,128)S(1)} %get-tuple-element.248), channel_id=1, source_target_pairs={{0,7},{1,6},{2,5},{3,4},{4,3},{5,2},{6,1},{7,0},{8,15},{9,14},{10,... | collective-permute-start | bytes 968 | tf_op jit(solution)/shard_map/ppermute | solution.py:133
  109.9 6.7 %collective-permute-start.10 = (f32[1,80]{1,0:T(1,128)S(1)}, f32[1,80]{1,0:T(1,128)S(1)}, u32[]{:S(2)}, u32[]{:S(2)}) collective-permute-start(f32[1,80]{1,0:T(1,128)S(1)} %get-tuple-element.247), channel_id=1, source_target_pairs={{0,8},{1,9},{2,10},{3,11},{4,12},{5,13},{6,14},{7,15},{8,0},{9,1},... | collective-permute-start | bytes 968 | tf_op jit(solution)/shard_map/ppermute | solution.py:133
  110.4 9.6 %collective-permute-start.11 = (f32[1,80]{1,0:T(1,128)S(1)}, f32[1,80]{1,0:T(1,128)S(1)}, u32[]{:S(2)}, u32[]{:S(2)}) collective-permute-start(f32[1,80]{1,0:T(1,128)S(1)} %get-tuple-element.246), channel_id=1, source_target_pairs={{0,9},{1,8},{2,11},{3,10},{4,13},{5,12},{6,15},{7,14},{8,1},{9,0},... | collective-permute-start | bytes 968 | tf_op jit(solution)/shard_map/ppermute | solution.py:133
  112.8 7.8 %collective-permute-start.12 = (f32[1,80]{1,0:T(1,128)S(1)}, f32[1,80]{1,0:T(1,128)S(1)}, u32[]{:S(2)}, u32[]{:S(2)}) collective-permute-start(f32[1,80]{1,0:T(1,128)S(1)} %get-tuple-element.245), channel_id=1, source_target_pairs={{0,10},{1,11},{2,8},{3,9},{4,14},{5,15},{6,12},{7,13},{8,2},{9,3},... | collective-permute-start | bytes 968 | tf_op jit(solution)/shard_map/ppermute | solution.py:133
  113.4 10.7 %collective-permute-start.13 = (f32[1,80]{1,0:T(1,128)S(1)}, f32[1,80]{1,0:T(1,128)S(1)}, u32[]{:S(2)}, u32[]{:S(2)}) collective-permute-start(f32[1,80]{1,0:T(1,128)S(1)} %get-tuple-element.244), channel_id=1, source_target_pairs={{0,11},{1,10},{2,9},{3,8},{4,15},{5,14},{6,13},{7,12},{8,3},{9,2},... | collective-permute-start | bytes 968 | tf_op jit(solution)/shard_map/ppermute | solution.py:133
  116.1 8.0 %collective-permute-start.14 = (f32[1,80]{1,0:T(1,128)S(1)}, f32[1,80]{1,0:T(1,128)S(1)}, u32[]{:S(2)}, u32[]{:S(2)}) collective-permute-start(f32[1,80]{1,0:T(1,128)S(1)} %get-tuple-element.243), channel_id=1, source_target_pairs={{0,12},{1,13},{2,14},{3,15},{4,8},{5,9},{6,10},{7,11},{8,4},{9,5},... | collective-permute-start | bytes 968 | tf_op jit(solution)/shard_map/ppermute | solution.py:133
  116.6 7.5 %collective-permute-start.15 = (f32[1,80]{1,0:T(1,128)S(1)}, f32[1,80]{1,0:T(1,128)S(1)}, u32[]{:S(2)}, u32[]{:S(2)}) collective-permute-start(f32[1,80]{1,0:T(1,128)S(1)} %get-tuple-element.242), channel_id=1, source_target_pairs={{0,13},{1,12},{2,15},{3,14},{4,9},{5,8},{6,11},{7,10},{8,5},{9,4},... | collective-permute-start | bytes 968 | tf_op jit(solution)/shard_map/ppermute | solution.py:133
  119.9 6.3 %collective-permute-start.16 = (f32[1,80]{1,0:T(1,128)S(1)}, f32[1,80]{1,0:T(1,128)S(1)}, u32[]{:S(2)}, u32[]{:S(2)}) collective-permute-start(f32[1,80]{1,0:T(1,128)S(1)} %get-tuple-element.241), channel_id=1, source_target_pairs={{0,14},{1,15},{2,12},{3,13},{4,10},{5,11},{6,8},{7,9},{8,6},{9,7},... | collective-permute-start | bytes 968 | tf_op jit(solution)/shard_map/ppermute | solution.py:133
  120.6 5.7 %collective-permute-start.17 = (f32[1,80]{1,0:T(1,128)S(1)}, f32[1,80]{1,0:T(1,128)S(1)}, u32[]{:S(2)}, u32[]{:S(2)}) collective-permute-start(f32[1,80]{1,0:T(1,128)S(1)} %get-tuple-element.240), channel_id=1, source_target_pairs={{0,15},{1,14},{2,13},{3,12},{4,11},{5,10},{6,9},{7,8},{8,7},{9,6},... | collective-permute-start | bytes 968 | tf_op jit(solution)/shard_map/ppermute | solution.py:133
